TPU v7x, 256 devices: a whole 4x4x8 slice. The times are simulated.
256 devices in a mesh: filt: 2 (over core), row: 4 (over x), col: 32 (over z, y).
Axes of the slice: x: 4, y: 4, z: 8, core: 2. Of those that a mesh axis runs over, the one named last changes fastest.
Arguments:
- particles: bfloat16 [24576, 256], P(('filt', 'row', 'col')), parts along dimension 0, may hold values from -6 to 6
- cotangent: bfloat16 [24576, 256], P(('filt', 'row', 'col')), parts along dimension 0, may hold values from -3 to 3
- row_potential: bfloat16 [24576], P(('filt', 'row', 'col')), parts along dimension 0, may hold values from -0.099609375 to 0.099609375
- col_potential: bfloat16 [24576], P(('filt', 'row', 'col')), parts along dimension 0, may hold values from -0.099609375 to 0.099609375
- weights: bfloat16 [24576], P(('filt', 'row', 'col')), parts along dimension 0, may hold values from 0.5 to 18
Outputs:
- grad_particles: bfloat16 [24576, 256], P(('filt', 'row', 'col')), parts along dimension 0
- grad_weights: float32 [24576], P(('filt', 'row', 'col')), parts along dimension 0
There are 2 independent parts, one for each index of `filt`. A program takes and returns all parts, laid end to end along the dimension named above; each array names one. Nothing has to cross between parts.
All inputs are finite; a program needn't handle non-finite values.
Results may differ from a plain program's by a relative error of at most 0.02.
Values may be sent and summed in bfloat16 or wider, within the bound.
No kernel may reach another device: no remote copies, remote signals or barrier semaphores. Data moves between devices by JAX's collectives and lax.ppermute only.
A program may use at most 64 MiB of HBM per device.

v0:
```python
import jax
import jax.numpy as jnp
from jax import lax
from jax.sharding import PartitionSpec as P

ITERS = 4
EPS = 0.09


def local(particles, cotangent, row_potential, col_potential, weights):
    row_parts, row_fpot, row_wts = (
        lax.all_gather(particles, "col", axis=0, tiled=True),
        lax.all_gather(row_potential, "col", axis=0, tiled=True),
        lax.all_gather(weights, "col", axis=0, tiled=True),
    )
    col_parts, col_grads, col_gpot = (
        lax.all_gather(particles, "row", axis=0, tiled=True),
        lax.all_gather(cotangent, "row", axis=0, tiled=True),
        lax.all_gather(col_potential, "row", axis=0, tiled=True),
    )
    own = particles.shape[0]
    width = particles.shape[1]
    rows = row_parts.shape[0]
    cols = col_parts.shape[0]
    blk = 512
    count = rows // blk
    row_float = row_parts.astype(jnp.float32)
    row_sq = jnp.sum(row_float * row_float, axis=1)
    col_float = col_parts.astype(jnp.float32)
    col_sq = jnp.sum(col_float * col_float, axis=1)
    fpot = row_fpot.astype(jnp.float32)
    gpot = col_gpot.astype(jnp.float32)
    stacked = jnp.concatenate([col_parts, col_grads], axis=0)
    items = (
        row_parts.reshape(count, blk, width),
        fpot.reshape(count, blk),
        row_sq.reshape(count, blk),
    )

    def plan_from(cross, pot_blk, sq_blk):
        cost = (sq_blk[:, None] + col_sq[None, :] - 2.0 * cross) / (2.0 * width)
        return jnp.exp((pot_blk[:, None] + gpot[None, :] - cost) / EPS)

    def plan_only(part_blk, pot_blk, sq_blk):
        cross = jnp.einsum("rd,cd->rc", part_blk, col_parts, preferred_element_type=jnp.float32)
        return plan_from(cross, pot_blk, sq_blk)

    def first(carry, item):
        part_blk, pot_blk, sq_blk = item
        both = jnp.einsum("rd,cd->rc", part_blk, stacked, preferred_element_type=jnp.float32)
        plan = plan_from(both[:, :cols], pot_blk, sq_blk)
        weighted = plan * both[:, cols:]
        return (
            (carry[0] + jnp.sum(plan, axis=0), carry[1] + jnp.sum(weighted, axis=0)),
            (jnp.sum(plan, axis=1), jnp.sum(weighted, axis=1)),
        )

    zeros_c = jnp.zeros((cols,), jnp.float32)
    (colmass_part, colph_part), (rowmass_part, rowph_part) = lax.scan(
        first, (zeros_c, zeros_c), items
    )
    rowmass, rowph = lax.psum((rowmass_part.reshape(rows), rowph_part.reshape(rows)), "col")
    colmass, colph = lax.psum((colmass_part, colph_part), "row")
    psi = zeros_c
    phi = jnp.zeros((rows,), jnp.float32)
    for step in range(ITERS):

        def apply_rows(carry, item):
            plan = plan_only(item[0], item[1], item[2])
            return (carry, jnp.dot(plan, psi, precision=lax.Precision.HIGHEST))

        unused, row_apply = lax.scan(apply_rows, jnp.zeros((), jnp.float32), items)
        row_total = lax.psum(row_apply.reshape(rows), "col")
        phi = -(rowph + row_total) / rowmass

        def apply_cols(acc, item):
            plan = plan_only(item[0], item[1], item[2])
            return (acc + jnp.dot(item[3], plan, precision=lax.Precision.HIGHEST), None)

        col_apply, unused_out = lax.scan(apply_cols, zeros_c, items + (phi.reshape(count, blk),))
        col_total = lax.psum(col_apply, "row")
        psi = -(colph + col_total) / colmass

    def last(acc, item):
        part_blk, pot_blk, sq_blk, phi_blk = item
        both = jnp.einsum("rd,cd->rc", part_blk, stacked, preferred_element_type=jnp.float32)
        plan = plan_from(both[:, :cols], pot_blk, sq_blk)
        mixed = plan * (both[:, cols:] + phi_blk[:, None] + psi[None, :])
        qrow = jnp.sum(mixed, axis=1)
        plan_bf = plan.astype(jnp.bfloat16)
        mixed_bf = mixed.astype(jnp.bfloat16)
        rowterm = jnp.dot(plan_bf, col_grads, preferred_element_type=jnp.float32)
        rowterm = rowterm + (
            jnp.dot(mixed_bf, col_parts, preferred_element_type=jnp.float32)
            - qrow[:, None] * part_blk.astype(jnp.float32)
        ) / (width * EPS)
        return (
            acc + jnp.einsum("rc,rd->cd", mixed_bf, part_blk, preferred_element_type=jnp.float32),
            rowterm,
        )

    col_acc, row_terms = lax.scan(
        last, jnp.zeros((cols, width), jnp.float32), items + (phi.reshape(count, blk),)
    )
    row_terms = row_terms.reshape(rows, width)
    start = lax.axis_index("col") * own
    summed = lax.psum(row_terms.astype(jnp.bfloat16), "col").astype(jnp.float32)
    row_own = lax.dynamic_slice_in_dim(summed, start, own, 0)
    col_own = lax.psum_scatter(
        col_acc.astype(jnp.bfloat16), "row", scatter_dimension=0, tiled=True
    ).astype(jnp.float32)
    grad_particles = (row_own + col_own / (width * EPS)).astype(jnp.bfloat16)
    phi_own = lax.dynamic_slice_in_dim(phi, start, own, 0)
    own_wts = weights.astype(jnp.float32)
    total, wphi = lax.psum((jnp.sum(own_wts), jnp.sum(own_wts * phi_own)), ("row", "col"))
    count_all = rows * lax.axis_size("row")
    grad_weights = -(count_all / total) * (phi_own - wphi / total)
    return (grad_particles, grad_weights)


def solution(mesh):
    return jax.shard_map(
        local,
        mesh=mesh,
        in_specs=(
            P(("filt", "row", "col"), None),
            P(("filt", "row", "col"), None),
            P(("filt", "row", "col")),
            P(("filt", "row", "col")),
            P(("filt", "row", "col")),
        ),
        out_specs=(P(("filt", "row", "col"), None), P(("filt", "row", "col"))),
        check_vma=False,
    )
```

profile of v0, /device:TPU:8, one launch (start us, length us, event | category | flops | bytes accessed | tf_op | source)
XLA Modules:
  0.0 1151.9 jit_solution(2241112115767740689)
XLA Ops:
  7.2 0.7 all-gather.2.cloned.1.call-update
  8.0 1.3 dynamic-slice
  9.9 0.9 dynamic-update-slice
  10.7 75.0 %all-reduce = bf16[3072]{0:T(1024)(128)(2,1)S(1)} all-reduce(bf16[3072]{0:T(1024)(128)(2,1)S(1)} %dynamic-update-slice), channel_id=1, replica_groups=mesh['filt'=2,'row'=4,'col'=32] {'col'}, use_global_device_ids=true, to_apply=%add | all-reduce | flops 3072 | bytes 12288
  85.8 1.3 dynamic-slice.1
  87.6 0.9 dynamic-update-slice.1
  88.5 10.5 all-reduce.1
  99.0 12.3 %all_gather.18 = bf16[384,256]{1,0:T(8,128)(2,1)S(1)} all-gather(bf16[96,256]{1,0:T(8,128)(2,1)} %param.25), channel_id=1, replica_groups=mesh['filt'=2,'row'=4,'col'=32] {'row'}, dimensions={0}, use_global_device_ids=true | all-gather | bytes 245760 | tf_op jit(solution)/shard_map/all_gather | solution.py:17
  111.3 12.3 %all_gather.19 = bf16[384,256]{1,0:T(8,128)(2,1)S(1)} all-gather(bf16[96,256]{1,0:T(8,128)(2,1)} %param.26), channel_id=1, replica_groups=mesh['filt'=2,'row'=4,'col'=32] {'row'}, dimensions={0}, use_global_device_ids=true | all-gather | bytes 245760 | tf_op jit(solution)/shard_map/all_gather | solution.py:18
  123.9 2.0 multiply_reduce_fusion
  125.9 7.0 while.118
  132.9 7.5 while.117
  133.4 0.8 fusion.226
  134.6 0.8 fusion.226
  135.9 0.8 fusion.226
  137.1 0.8 fusion.226
  138.4 0.8 fusion.226
  139.6 0.8 fusion.226
  140.5 139.2 %all-reduce.3 = (f32[3072]{0:T(1024)S(1)}, f32[3072]{0:T(1024)S(1)}, f32[3072]{0:T(1024)S(1)}) all-reduce(f32[3072]{0:T(1024)S(1)} %reshape.119, f32[3072]{0:T(1024)S(1)} %reshape.117, f32[3072]{0:T(1024)S(1)} %reshape.118), channel_id=1, replica_groups=mesh['filt'=2,'row'=4,'col'=32] {'col'}, use_global_device_ids=true, to_apply=%region_13.14 | all-reduce | flops 9216 | bytes 73728 | tf_op jit(solution)/shard_map/psum | solution.py:62
  279.7 5.8 while.119
  285.5 7.9 all-reduce.4
  294.0 7.5 while.124
  294.4 0.8 fusion.268
  295.6 0.8 fusion.268
  296.9 0.8 fusion.268
  298.1 0.8 fusion.268
  299.4 0.8 fusion.268
  300.6 0.8 fusion.268
  301.5 137.7 %psum.111 = f32[3072]{0:T(1024)S(1)} all-reduce(f32[3072]{0:T(1024)S(1)} %reshape.121), channel_id=1, replica_groups=mesh['filt'=2,'row'=4,'col'=32] {'col'}, use_global_device_ids=true, to_apply=%region_20.21 | all-reduce | flops 3072 | bytes 24576 | tf_op jit(solution)/shard_map/psum | solution.py:73
  439.2 5.8 while.120
  445.0 9.7 psum.112
  455.3 7.5 while.125
  455.7 0.8 fusion.274
  456.9 0.8 fusion.274
  458.2 0.8 fusion.274
  459.5 0.8 fusion.274
  460.7 0.8 fusion.274
  462.0 0.8 fusion.274
  462.8 137.7 %psum.113 = f32[3072]{0:T(1024)S(1)} all-reduce(f32[3072]{0:T(1024)S(1)} %reshape.123), channel_id=1, replica_groups=mesh['filt'=2,'row'=4,'col'=32] {'col'}, use_global_device_ids=true, to_apply=%region_26.27 | all-reduce | flops 3072 | bytes 24576 | tf_op jit(solution)/shard_map/psum | solution.py:73
  600.5 5.8 while.121
  606.3 7.7 psum.114
  614.7 7.5 while.126
  615.1 0.8 fusion.280
  616.3 0.8 fusion.280
  617.6 0.8 fusion.280
  618.8 0.8 fusion.280
  620.1 0.8 fusion.280
  621.3 0.8 fusion.280
  622.2 138.0 %psum.115 = f32[3072]{0:T(1024)S(1)} all-reduce(f32[3072]{0:T(1024)S(1)} %reshape.125), channel_id=1, replica_groups=mesh['filt'=2,'row'=4,'col'=32] {'col'}, use_global_device_ids=true, to_apply=%region_32.33 | all-reduce | flops 3072 | bytes 24576 | tf_op jit(solution)/shard_map/psum | solution.py:73
  760.2 5.8 while.122
  765.9 9.7 psum.116
  775.7 16.9 %while.123 = (s32[]{:T(128)}, f32[384,256]{1,0:T(8,128)S(1)}, bf16[6,512,256]{2,1,0:T(8,128)(2,1)}, f32[6,512]{1,0:T(8,128)S(1)}, f32[384]{0:T(512)S(1)}, /*inde...) while((s32[]{:T(128)}, f32[384,256]{1,0:T(8,128)S(1)}, ...), condition=%wide.region_38.39_spmd.clone, body=%wide.region_36.38_spmd.clone.sunk | while | flops 508100096 | bytes 9079975 | solution.py:102
  777.1 1.0 fusion.262
  779.9 1.0 fusion.262
  782.7 1.0 fusion.262
  785.5 1.0 fusion.262
  788.4 1.0 fusion.262
  791.2 1.0 fusion.262
  792.6 0.7 convert_element_type.46
  793.4 0.7 all-reduce.7.cloned.1.call-update
  794.1 0.7 convert_reduce_fusion
  794.8 346.5 %all-reduce.2 = (f32[]{:T(128)}, f32[]{:T(128)}) all-reduce(f32[]{:T(128)} %get-tuple-element.718, f32[]{:T(128)} %get-tuple-element.717), channel_id=1, replica_groups=mesh['filt'=2,'row'=4,'col'=32] {'row','col'}, use_global_device_ids=true, to_apply=%region_44.45 | all-reduce | flops 2 | bytes 16 | tf_op jit(solution)/shard_map/psum | solution.py:115
  1143.3 0.6 subtract_multiply_fusion
  1143.9 1.5 add_convert_fusion
  (306 shorter events, 52.6 us)
Async XLA Ops:
  7.2 116.7 %all-gather.2.cloned.1.call-start = ((), (), s32[]{:S(2)}) async-start(), calls=%async_computation.1 | async-start | bytes 1622016 | tf_op jit(solution)/shard_map/all_gather | solution.py:12
  7.9 1136.0 %reduce-scatter.2.cloned.1.call-start = ((), (), s32[]{:S(2)}) async-start(), calls=%async_computation.3 | async-start | bytes 245760 | tf_op jit(solution)/shard_map/reduce_scatter | solution.py:109
  123.8 2.1 copy-start
  293.4 0.6 copy-start.2
  454.7 0.6 copy-start.3
  614.1 0.6 copy-start.1
  792.6 1.5 copy-start.4
  793.4 350.6 %all-reduce.7.cloned.1.call-start = ((), (), s32[]{:S(2)}) async-start(), calls=%async_computation.2 | async-start | bytes 3145728 | tf_op jit(solution)/shard_map/psum | solution.py:107
Sparse Core Ops, SparseCore 0:
  10.6 78.8 all-gather.1
  793.5 18.2 reduce-scatter.1
  815.6 149.9 all-reduce.6
where the time goes:
time: 1150 us
  blocking collectives  1040 us (90%)
  matrix products  65.2 us (6%)
  between operations  17.3 us (2%)
  other arithmetic  12.4 us (1%)
    psum x3, blocking collectives, local(): row_total = lax.psum(row_apply.reshape(rows), 'col')  413 us
    psum x1, blocking collectives, local(): lax.psum((jnp.sum(own_wts), jnp.sum(own_wts * phi_own)), ('row', 'col'))  347 us
    psum x1, blocking collectives, local(): lax.psum((rowmass_part.reshape(rows), rowph_part.reshape(rows)), 'col')  139 us
    unnamed x2, blocking collectives  85.5 us
    psum x3, blocking collectives, local(): col_total = lax.psum(col_apply, 'row')  27.2 us
  transfers between devices with their start and end apart: 3, of which 0 were waited for; matrix products, arithmetic and copies ran while one was open for 0% of the time, Pallas kernels for 0%

commit v1 on v0

--- a/solution.py
+++ b/solution.py
@@ -112,7 +112,7 @@
     grad_particles = (row_own + col_own / (width * EPS)).astype(jnp.bfloat16)
     phi_own = lax.dynamic_slice_in_dim(phi, start, own, 0)
     own_wts = weights.astype(jnp.float32)
-    total, wphi = lax.psum((jnp.sum(own_wts), jnp.sum(own_wts * phi_own)), ("row", "col"))
+    total, wphi = lax.psum(lax.psum((jnp.sum(own_wts), jnp.sum(own_wts * phi_own)), "col"), "row")
     count_all = rows * lax.axis_size("row")
     grad_weights = -(count_all / total) * (phi_own - wphi / total)
     return (grad_particles, grad_weights)

time: 1150 us -> 1050 us (0.913)
  blocking collectives: 1040 us -> 772 us
  waiting for transfers between devices: 1.4 us -> 168 us
    psum x1, blocking collectives: 347 us -> 73.6 us  [local(): lax.psum((jnp.sum(own_wts), jnp.sum(own_wts * phi_own)), 'col')]
    psum x1, waiting for transfers between devices: 0.01 us -> 154 us  [local(): summed = lax.psum(row_terms.astype(jnp.bfloat16), 'col').astype(jnp.float32)]
    reduce_scatter x1, waiting for transfers between devices: 0.01 us -> 13.2 us  [local(): lax.psum_scatter(col_acc.astype(jnp.bfloat16), 'row', scatter_dimension=0...]
  transfers between devices with their start and end apart: 3 -> 3, of which waited for: 0 -> 2; matrix products, arithmetic and copies ran while one was open for 0% -> 0% of each run, Pallas kernels for 0% -> 0%
where the time goes in v1:
time: 1050 us
  blocking collectives  772 us (74%)
  waiting for transfers between devices  168 us (16%)
  matrix products  65.3 us (6%)
  between operations  17.3 us (2%)
  other arithmetic  12.4 us (1%)
    psum x3, blocking collectives, local(): row_total = lax.psum(row_apply.reshape(rows), 'col')  413 us
    psum x1, waiting for transfers between devices, local(): summed = lax.psum(row_terms.astype(jnp.bfloat16), 'col').astype(jnp.float32)  154 us
    psum x1, blocking collectives, local(): lax.psum((rowmass_part.reshape(rows), rowph_part.reshape(rows)), 'col')  139 us
    unnamed x2, blocking collectives  85.5 us
    psum x1, blocking collectives, local(): lax.psum((jnp.sum(own_wts), jnp.sum(own_wts * phi_own)), 'col')  73.6 us
    psum x3, blocking collectives, local(): col_total = lax.psum(col_apply, 'row')  27.9 us
  transfers between devices with their start and end apart: 3, of which 2 were waited for; matrix products, arithmetic and copies ran while one was open for 0% of the time, Pallas kernels for 0%

profile of v1, /device:TPU:8, one launch (start us, length us, event | category | flops | bytes accessed | tf_op | source)
XLA Modules:
  0.0 1046.8 jit_solution(6686094433089010969)
XLA Ops:
  7.2 0.7 all-gather.2.cloned.1.call-update
  8.0 1.3 dynamic-slice
  9.9 0.9 dynamic-update-slice
  10.7 75.0 %all-reduce = bf16[3072]{0:T(1024)(128)(2,1)S(1)} all-reduce(bf16[3072]{0:T(1024)(128)(2,1)S(1)} %dynamic-update-slice), channel_id=1, replica_groups=mesh['filt'=2,'row'=4,'col'=32] {'col'}, use_global_device_ids=true, to_apply=%add | all-reduce | flops 3072 | bytes 12288
  85.8 1.3 dynamic-slice.1
  87.6 0.9 dynamic-update-slice.1
  88.5 10.5 %all-reduce.1 = bf16[384]{0:T(512)(128)(2,1)S(1)} all-reduce(bf16[384]{0:T(512)(128)(2,1)S(1)} %dynamic-update-slice.1), channel_id=1, replica_groups=mesh['filt'=2,'row'=4,'col'=32] {'row'}, use_global_device_ids=true, to_apply=%add.1 | all-reduce | flops 384 | bytes 1536
  99.0 12.3 %all_gather.18 = bf16[384,256]{1,0:T(8,128)(2,1)S(1)} all-gather(bf16[96,256]{1,0:T(8,128)(2,1)} %param.25), channel_id=1, replica_groups=mesh['filt'=2,'row'=4,'col'=32] {'row'}, dimensions={0}, use_global_device_ids=true | all-gather | bytes 245760 | tf_op jit(solution)/shard_map/all_gather | solution.py:17
  111.3 12.3 %all_gather.19 = bf16[384,256]{1,0:T(8,128)(2,1)S(1)} all-gather(bf16[96,256]{1,0:T(8,128)(2,1)} %param.26), channel_id=1, replica_groups=mesh['filt'=2,'row'=4,'col'=32] {'row'}, dimensions={0}, use_global_device_ids=true | all-gather | bytes 245760 | tf_op jit(solution)/shard_map/all_gather | solution.py:18
  123.9 2.0 multiply_reduce_fusion
  125.9 7.0 while.118
  132.9 7.5 while.117
  133.4 0.8 fusion.226
  134.6 0.8 fusion.226
  135.9 0.8 fusion.226
  137.1 0.8 fusion.226
  138.4 0.8 fusion.226
  139.6 0.8 fusion.226
  140.5 139.2 %all-reduce.3 = (f32[3072]{0:T(1024)S(1)}, f32[3072]{0:T(1024)S(1)}, f32[3072]{0:T(1024)S(1)}) all-reduce(f32[3072]{0:T(1024)S(1)} %reshape.119, f32[3072]{0:T(1024)S(1)} %reshape.117, f32[3072]{0:T(1024)S(1)} %reshape.118), channel_id=1, replica_groups=mesh['filt'=2,'row'=4,'col'=32] {'col'}, use_global_device_ids=true, to_apply=%region_13.14 | all-reduce | flops 9216 | bytes 73728 | tf_op jit(solution)/shard_map/psum | solution.py:62
  279.7 5.8 while.119
  285.5 7.9 all-reduce.5
  294.0 7.5 while.124
  294.4 0.8 fusion.268
  295.6 0.8 fusion.268
  296.9 0.8 fusion.268
  298.1 0.8 fusion.268
  299.4 0.8 fusion.268
  300.6 0.8 fusion.268
  301.5 137.7 %psum.125 = f32[3072]{0:T(1024)S(1)} all-reduce(f32[3072]{0:T(1024)S(1)} %reshape.121), channel_id=1, replica_groups=mesh['filt'=2,'row'=4,'col'=32] {'col'}, use_global_device_ids=true, to_apply=%region_20.21 | all-reduce | flops 3072 | bytes 24576 | tf_op jit(solution)/shard_map/psum | solution.py:73
  439.2 5.8 while.120
  445.0 9.7 psum.126
  455.3 7.5 while.125
  455.7 0.8 fusion.274
  457.0 0.8 fusion.274
  458.2 0.8 fusion.274
  459.5 0.8 fusion.274
  460.7 0.8 fusion.274
  462.0 0.8 fusion.274
  462.8 137.7 %psum.127 = f32[3072]{0:T(1024)S(1)} all-reduce(f32[3072]{0:T(1024)S(1)} %reshape.123), channel_id=1, replica_groups=mesh['filt'=2,'row'=4,'col'=32] {'col'}, use_global_device_ids=true, to_apply=%region_26.27 | all-reduce | flops 3072 | bytes 24576 | tf_op jit(solution)/shard_map/psum | solution.py:73
  600.5 5.8 while.121
  606.4 7.7 psum.128
  614.7 7.5 while.126
  615.1 0.8 fusion.280
  616.4 0.8 fusion.280
  617.6 0.8 fusion.280
  618.9 0.8 fusion.280
  620.1 0.8 fusion.280
  621.4 0.8 fusion.280
  622.2 137.9 %psum.129 = f32[3072]{0:T(1024)S(1)} all-reduce(f32[3072]{0:T(1024)S(1)} %reshape.125), channel_id=1, replica_groups=mesh['filt'=2,'row'=4,'col'=32] {'col'}, use_global_device_ids=true, to_apply=%region_32.33 | all-reduce | flops 3072 | bytes 24576 | tf_op jit(solution)/shard_map/psum | solution.py:73
  760.1 5.8 while.122
  765.9 0.7 convert_reduce_fusion
  766.7 73.6 %all-reduce.2 = (f32[]{:T(128)}, f32[]{:T(128)}) all-reduce(f32[]{:T(128)} %get-tuple-element.718, f32[]{:T(128)} %get-tuple-element.717), channel_id=1, replica_groups=mesh['filt'=2,'row'=4,'col'=32] {'col'}, use_global_device_ids=true, to_apply=%region_45.46 | all-reduce | flops 2 | bytes 16 | tf_op jit(solution)/shard_map/psum | solution.py:115
  840.3 10.4 all-reduce.4
  850.7 16.9 %while.123 = (s32[]{:T(128)}, f32[384,256]{1,0:T(8,128)S(1)}, bf16[6,512,256]{2,1,0:T(8,128)(2,1)}, f32[6,512]{1,0:T(8,128)S(1)}, f32[384]{0:T(512)S(1)}, /*inde...) while((s32[]{:T(128)}, f32[384,256]{1,0:T(8,128)S(1)}, ...), condition=%wide.region_38.39_spmd.clone, body=%wide.region_36.38_spmd.clone.sunk | while | flops 508100096 | bytes 9079975 | solution.py:102
  852.1 1.0 fusion.262
  854.9 1.0 fusion.262
  857.7 1.0 fusion.262
  860.6 1.0 fusion.262
  863.4 1.0 fusion.262
  866.2 1.0 fusion.262
  867.6 0.7 convert_element_type.46
  871.7 13.2 %reduce-scatter.2.cloned.1.call-done = bf16[96,256]{1,0:T(8,128)(2,1)} async-done(((bf16[384,256]{1,0:T(8,128)(2,1)}), bf16[96,256]{1,0:T(8,128)(2,1)}) %reduce-scatter.2.cloned.1.call-update) | async-done | bytes 49168 | tf_op jit(solution)/shard_map/reduce_scatter | solution.py:109
  884.9 153.9 %all-reduce.8.cloned.1.call-done = bf16[3072,256]{1,0:T(8,128)(2,1)} async-done(((bf16[3072,256]{1,0:T(8,128)(2,1)}), bf16[3072,256]{1,0:T(8,128)(2,1)}) %all-reduce.8.cloned.1.call-update) | async-done | bytes 1572880 | tf_op jit(solution)/shard_map/psum | solution.py:107
  1038.8 1.5 add_convert_fusion
  (306 shorter events, 53.9 us)
Async XLA Ops:
  7.2 116.7 %all-gather.2.cloned.1.call-start = ((), (), s32[]{:S(2)}) async-start(), calls=%async_computation.1 | async-start | bytes 1622016 | tf_op jit(solution)/shard_map/all_gather | solution.py:12
  7.9 877.0 %reduce-scatter.2.cloned.1.call-start = ((), (), s32[]{:S(2)}) async-start(), calls=%async_computation.3 | async-start | bytes 245760 | tf_op jit(solution)/shard_map/reduce_scatter | solution.py:109
  123.9 2.1 copy-start
  293.4 0.6 copy-start.2
  454.7 0.6 copy-start.3
  614.1 0.6 copy-start.1
  760.1 5.8 copy-start.4
  868.4 170.4 %all-reduce.8.cloned.1.call-start = ((), (), s32[]{:S(2)}) async-start(), calls=%async_computation.2 | async-start | bytes 3145728 | tf_op jit(solution)/shard_map/psum | solution.py:107
Sparse Core Ops, SparseCore 0:
  10.6 78.8 all-gather.1
  868.5 16.3 reduce-scatter.1
  888.7 150.0 all-reduce.7
